TPU v7x, 256 devices: a whole 4x4x8 slice. The times are simulated.
256 devices in a mesh: task: 8 (over z_hi, core), row: 8 (over x, z_lo), col: 4 (over y).
Axes of the slice: x: 4, y: 4, z: 8 (z_hi: 4, z_lo: 2; z = z_hi * 2 + z_lo), core: 2. Of those that a mesh axis runs over, the one named last changes fastest.
Arguments:
- activations: bfloat16 [8, 512, 13824], P('task', 'col', 'row'), may hold values from -6 to 6
- weights: bfloat16 [8, 13824, 5120], P('task', 'row', 'col'), may hold values from -0.0625 to 0.0625
- labels: int32 [8, 512], P('task'), may hold values from 0 to 127
- prototypes: bfloat16 [8, 128, 5120], P('task', None, 'col'), may hold values from -6 to 6
Outputs:
- merged: bfloat16 [13824, 5120], P('row', 'col')
- merged_out: bfloat16 [8, 512, 5120], P('task', 'row', 'col')
All inputs are finite; a program needn't handle non-finite values.
Results may differ from a plain program's by a relative error of at most 0.02.
Values may be sent and summed in bfloat16 or wider, within the bound.
A program may use at most 128 MiB of HBM per device.

v0:
```python
import jax
import jax.numpy as jnp
from jax import lax
from jax.sharding import PartitionSpec as P


def class_targets(label_rows, protos):
    count = label_rows.shape[0]
    onehot = (
        label_rows[:, None] == lax.broadcasted_iota(jnp.int32, (count, protos.shape[0]), 1)
    ).astype(jnp.bfloat16)
    return jnp.dot(onehot, protos, preferred_element_type=jnp.float32)


def local(activations, weights, labels, prototypes):
    acts = activations[0]
    weight = weights[0]
    label_row = labels[0]
    protos = prototypes[0]
    full_acts = lax.all_gather(acts, "col", axis=0, tiled=True)
    partial_out = jnp.dot(full_acts, weight, preferred_element_type=jnp.float32)
    output = lax.psum(partial_out.astype(jnp.bfloat16), "row").astype(jnp.float32)
    grad = output - class_targets(label_row, protos)
    gsq = (grad * grad).astype(jnp.bfloat16)
    wide = full_acts.astype(jnp.float32)
    asq = (wide * wide).astype(jnp.bfloat16)
    fisher = lax.dot_general(asq, gsq, (((0,), (0,)), ((), ())), preferred_element_type=jnp.float32)
    weighted = fisher * weight.astype(jnp.float32)
    numer, denom = (
        lax.psum_scatter(weighted, "task", scatter_dimension=0, tiled=True),
        lax.psum_scatter(fisher, "task", scatter_dimension=0, tiled=True),
    )
    piece = (numer / (denom + 1e-06)).astype(jnp.bfloat16)
    merged = lax.all_gather(piece, "task", axis=0, tiled=True)
    result = lax.psum_scatter(
        jnp.dot(full_acts, merged, preferred_element_type=jnp.float32).astype(jnp.bfloat16),
        "row",
        scatter_dimension=0,
        tiled=True,
    )
    return (merged, result[None])


def solution(mesh):
    placed = (
        P("task", "col", "row"),
        P("task", "row", "col"),
        P("task", None),
        P("task", None, "col"),
    )
    return jax.shard_map(
        local,
        mesh=mesh,
        in_specs=placed,
        out_specs=(P("row", "col"), P("task", "row", "col")),
        check_vma=False,
    )
```

profile of v0, /device:TPU:8, one launch (start us, length us, event | category | flops | bytes accessed | tf_op | source)
XLA Modules:
  0.0 475.8 jit_solution(1805810077636972893)
XLA Ops:
  7.2 0.0 copy-start
  7.2 0.0 all-gather.6.cloned.1.call-start
  7.2 0.7 all-gather.6.cloned.1.call-update
  7.9 0.0 copy-start.2
  7.9 0.0 all-reduce.2.cloned.1.call-start
  8.0 38.4 %all-gather.6.cloned.1.call-done = bf16[1,512,1728]{1,2,0:T(8,128)(2,1)} async-done(((bf16[1,128,1728]{1,2,0:T(8,128)(2,1)}), bf16[1,512,1728]{1,2,0:T(8,128)(2,1)}) %all-gather.6.cloned.1.call-update) | async-done | bytes 1769488 | tf_op jit(solution)/shard_map/all_gather | solution.py:20
  46.4 0.0 copy-start.1
  46.4 6.6 %fusion.4 = bf16[512,1280]{1,0:T(8,128)(2,1)} fusion(bf16[1,1728,1280]{2,1,0:T(8,128)(2,1)} %param.5, bf16[1,512,1728]{1,2,0:T(8,128)(2,1)} %all-gather.6.cloned.1.call-done), kind=kOutput, calls=%fused_computation.7 | convolution fusion | flops 2265579520 | bytes 7503872 | tf_op jit(solution)/shard_map/dot_general | solution.py:21
  53.0 0.0 all-reduce.2.cloned.1.call-update
  53.0 0.0 reduce-scatter.6.cloned.1.call-start
  53.1 90.5 %all-reduce.2.cloned.1.call-done = bf16[512,1280]{1,0:T(8,128)(2,1)} async-done(((bf16[512,1280]{1,0:T(8,128)(2,1)}), bf16[512,1280]{1,0:T(8,128)(2,1)}) %all-reduce.2.cloned.1.call-update) | async-done | bytes 1310736 | tf_op jit(solution)/shard_map/psum | solution.py:22
  143.6 0.0 copy-done
  143.6 0.0 copy-done.2
  143.6 0.0 copy-done.1
  143.6 9.8 %convert_multiply_fusion = (f32[1728,1280]{1,0:T(8,128)}, f32[1728,1280]{1,0:T(8,128)}) fusion(bf16[1,1728,1280]{2,1,0:T(8,128)(2,1)} %param.5, bf16[512,1280]{1,0:T(8,128)(2,1)} %all-reduce.2.cloned.1.call-done, bf16[1,128,1280]{2,1,0:T(8,128)(2,1)S(1)} %copy-done, s32[512]{0:T(512)S(1)} %bitcast.30, bf16[1,512,1728]{1,2,0:T(8,128)(2,1)S(1)} %copy-done.1), kind=kOutput, calls=%fused_computation | convolution fusion | flops 2442461184 | bytes 25528320 | tf_op jit(solution)/shard_map/dot_general | solution.py:27
  153.4 0.0 reduce-scatter.6.cloned.1.call-update
  153.4 0.0 reduce-scatter.8.cloned.1.call-start
  153.4 0.5 reduce-scatter.8.cloned.1.call-update
  154.0 0.0 all-gather.4.cloned.1.call-start
  154.0 96.8 %reduce-scatter.6.cloned.1.call-done = f32[216,1280]{1,0:T(8,128)} async-done(((f32[1728,1280]{1,0:T(8,128)}), f32[216,1280]{1,0:T(8,128)}) %reduce-scatter.6.cloned.1.call-update) | async-done | bytes 1105936 | tf_op jit(solution)/shard_map/reduce_scatter | solution.py:30
  250.8 104.8 %reduce-scatter.8.cloned.1.call-done = f32[216,1280]{1,0:T(8,128)} async-done(((f32[1728,1280]{1,0:T(8,128)}), f32[216,1280]{1,0:T(8,128)}) %reduce-scatter.8.cloned.1.call-update) | async-done | bytes 1105936 | tf_op jit(solution)/shard_map/reduce_scatter | solution.py:31
  355.7 2.5 divide_convert_fusion
  358.2 0.0 all-gather.4.cloned.1.call-update
  358.2 0.0 reduce-scatter.10.cloned.1.call-start
  358.3 54.9 %all-gather.4.cloned.1.call-done = bf16[1728,1280]{1,0:T(8,128)(2,1)} async-done(((bf16[216,1280]{1,0:T(8,128)(2,1)}), bf16[1728,1280]{1,0:T(8,128)(2,1)}) %all-gather.4.cloned.1.call-update) | async-done | bytes 4423696 | tf_op jit(solution)/shard_map/all_gather | solution.py:34
  413.1 4.8 %fusion.7 = bf16[512,1280]{0,1:T(8,128)(2,1)S(1)} fusion(bf16[1728,1280]{1,0:T(8,128)(2,1)} %all-gather.4.cloned.1.call-done, bf16[1,512,1728]{1,2,0:T(8,128)(2,1)S(1)} %copy-done.1), kind=kOutput, calls=%fused_computation.9 | convolution fusion | flops 2265579520 | bytes 7503872 | tf_op jit(solution)/shard_map/dot_general | solution.py:36
  418.0 1.4 copy.8
  419.4 0.0 reduce-scatter.10.cloned.1.call-update
  419.4 42.9 %reduce-scatter.10.cloned.1.call-done = bf16[64,1280]{1,0:T(8,128)(2,1)} async-done(((bf16[512,1280]{1,0:T(8,128)(2,1)}), bf16[64,1280]{1,0:T(8,128)(2,1)}) %reduce-scatter.10.cloned.1.call-update) | async-done | bytes 163856
  462.4 1.1 copy.9
  463.5 0.8 copy.7
  464.3 4.6 copy.12
Async XLA Ops:
  7.2 136.4 %copy-start = (bf16[1,128,1280]{2,1,0:T(8,128)(2,1)S(1)}, bf16[1,128,1280]{2,1,0:T(8,128)(2,1)}, u32[]{:S(2)}) copy-start(bf16[1,128,1280]{2,1,0:T(8,128)(2,1)} %param.7) | copy-start | bytes 983044
  7.2 39.2 %all-gather.6.cloned.1.call-start = ((), (), s32[]{:S(2)}) async-start(), calls=%async_computation.7 | async-start | bytes 2211840 | tf_op jit(solution)/shard_map/all_gather | solution.py:20
  7.9 135.7 %copy-start.2 = (s32[1,512]{1,0:T(1,128)S(1)}, s32[1,512]{1,0:T(1,128)}, u32[]{:S(2)}) copy-start(s32[1,512]{1,0:T(1,128)} %param.6) | copy-start | bytes 6148
  7.9 135.7 %all-reduce.2.cloned.1.call-start = ((), (), s32[]{:S(2)}) async-start(), calls=%async_computation.3 | async-start | bytes 2621440 | tf_op jit(solution)/shard_map/psum | solution.py:22
  46.4 97.2 %copy-start.1 = (bf16[1,512,1728]{1,2,0:T(8,128)(2,1)S(1)}, bf16[1,512,1728]{1,2,0:T(8,128)(2,1)}, u32[]{:S(2)}) copy-start(bf16[1,512,1728]{1,2,0:T(8,128)(2,1)} %all-gather.6.cloned.1.call-done) | copy-start | bytes 5308420
  53.0 197.8 %reduce-scatter.6.cloned.1.call-start = ((), (), s32[]{:S(2)}) async-start(), calls=%async_computation.4 | async-start | bytes 9953280 | tf_op jit(solution)/shard_map/reduce_scatter | solution.py:30
  153.4 202.3 %reduce-scatter.8.cloned.1.call-start = ((), (), s32[]{:S(2)}) async-start(), calls=%async_computation.5 | async-start | bytes 9953280 | tf_op jit(solution)/shard_map/reduce_scatter | solution.py:31
  154.0 259.2 %all-gather.4.cloned.1.call-start = ((), (), s32[]{:S(2)}) async-start(), calls=%async_computation.6 | async-start | bytes 4976640 | tf_op jit(solution)/shard_map/all_gather | solution.py:34
  358.2 104.1 %reduce-scatter.10.cloned.1.call-start = ((), (), s32[]{:S(2)}) async-start(), calls=%async_computation.8 | async-start | bytes 1474560
Sparse Core Ops, SparseCore 0:
  9.8 36.5 all-gather.5
  53.1 90.4 all-reduce.1
  153.5 97.2 reduce-scatter.5
  253.4 102.1 reduce-scatter.7
  358.3 54.7 all-gather.3
  419.6 42.7 reduce-scatter.9
where the time goes:
time: 476 us
  waiting for transfers between devices  430 us (90%)
  matrix products  21.2 us (4%)
  between operations  14.1 us (3%)
  local copies, waits for them, and re-layouts  8.06 us (2%)
    reduce_scatter x1, waiting for transfers between devices, local(): lax.psum_scatter(fisher, 'task', scatter_dimension=0, tiled=True)  105 us
    reduce_scatter x1, waiting for transfers between devices, local(): lax.psum_scatter(weighted, 'task', scatter_dimension=0, tiled=True)  96.8 us
    psum x1, waiting for transfers between devices, local(): lax.psum(partial_out.astype(jnp.bfloat16), 'row').astype(jnp.float32)  90.5 us
    all_gather x1, waiting for transfers between devices, local(): merged = lax.all_gather(piece, 'task', axis=0, tiled=True)  54.9 us
    unnamed x7, waiting for transfers between devices  44.2 us
    all_gather x1, waiting for transfers between devices, local(): full_acts = lax.all_gather(acts, 'col', axis=0, tiled=True)  38.4 us
    dot_general x1, matrix products, local(): lax.dot_general(asq, gsq, (((0,), (0,)), ((), ())), preferred_element_typ...  9.77 us
  transfers between devices with their start and end apart: 6, of which 6 were waited for; matrix products, arithmetic and copies ran while one was open for 0% of the time, Pallas kernels for 0%

commit v1 on v0

--- a/solution.py
+++ b/solution.py
@@ -31,7 +31,9 @@
         lax.psum_scatter(fisher, "task", scatter_dimension=0, tiled=True),
     )
     piece = (numer / (denom + 1e-06)).astype(jnp.bfloat16)
-    merged = lax.all_gather(piece, "task", axis=0, tiled=True)
+    merged = jnp.concatenate(
+        lax.all_to_all(jnp.stack([piece] * lax.axis_size("task")), "task", 0, 0), axis=0
+    )
     result = lax.psum_scatter(
         jnp.dot(full_acts, merged, preferred_element_type=jnp.float32).astype(jnp.bfloat16),
         "row",

time: 476 us -> 525 us (1.10)
  blocking collectives: 0 us -> 107 us
  waiting for transfers between devices: 430 us -> 373 us
    all_to_all x0 -> x1, blocking collectives: none -> 107 us  [local(): lax.all_to_all(jnp.stack([piece] * lax.axis_size('task')), 'task', 0, 0)]
    all_gather x1 -> x0, waiting for transfers between devices: 54.9 us -> none  [local(): merged = lax.all_gather(piece, 'task', axis=0, tiled=True)]
    unnamed x7 -> x6, waiting for transfers between devices: 44.2 us -> 42.4 us
  transfers between devices with their start and end apart: 6 -> 5, of which waited for: 6 -> 5; matrix products, arithmetic and copies ran while one was open for 0% -> 0% of each run, Pallas kernels for 0% -> 0%
where the time goes in v1:
time: 525 us
  waiting for transfers between devices  373 us (71%)
  blocking collectives  107 us (20%)
  matrix products  19 us (4%)
  between operations  13.8 us (3%)
  local copies, waits for them, and re-layouts  10.3 us (2%)
    all_to_all x1, blocking collectives, local(): lax.all_to_all(jnp.stack([piece] * lax.axis_size('task')), 'task', 0, 0)  107 us
    reduce_scatter x1, waiting for transfers between devices, local(): lax.psum_scatter(fisher, 'task', scatter_dimension=0, tiled=True)  105 us
    reduce_scatter x1, waiting for transfers between devices, local(): lax.psum_scatter(weighted, 'task', scatter_dimension=0, tiled=True)  96.8 us
    psum x1, waiting for transfers between devices, local(): lax.psum(partial_out.astype(jnp.bfloat16), 'row').astype(jnp.float32)  90.5 us
    unnamed x6, waiting for transfers between devices  42.4 us
    all_gather x1, waiting for transfers between devices, local(): full_acts = lax.all_gather(acts, 'col', axis=0, tiled=True)  38.4 us
  transfers between devices with their start and end apart: 5, of which 5 were waited for; matrix products, arithmetic and copies ran while one was open for 0% of the time, Pallas kernels for 0%

profile of v1, /device:TPU:8, one launch (start us, length us, event | category | flops | bytes accessed | tf_op | source)
XLA Modules:
  0.0 524.7 jit_solution(12576227571012848471)
XLA Ops:
  7.2 0.0 copy-start
  7.2 0.0 all-gather.3.cloned.1.call-start
  7.2 0.7 all-gather.3.cloned.1.call-update
  7.9 0.0 copy-start.3
  7.9 0.0 all-reduce.2.cloned.1.call-start
  8.0 38.4 %all-gather.3.cloned.1.call-done = bf16[1,512,1728]{1,2,0:T(8,128)(2,1)} async-done(((bf16[1,128,1728]{1,2,0:T(8,128)(2,1)}), bf16[1,512,1728]{1,2,0:T(8,128)(2,1)}) %all-gather.3.cloned.1.call-update) | async-done | bytes 1769488 | tf_op jit(solution)/shard_map/all_gather | solution.py:20
  46.4 0.0 copy-start.2
  46.4 6.6 %fusion.4 = bf16[512,1280]{1,0:T(8,128)(2,1)} fusion(bf16[1,1728,1280]{2,1,0:T(8,128)(2,1)} %param.5, bf16[1,512,1728]{1,2,0:T(8,128)(2,1)} %all-gather.3.cloned.1.call-done), kind=kOutput, calls=%fused_computation.7 | convolution fusion | flops 2265579520 | bytes 7503872 | tf_op jit(solution)/shard_map/dot_general | solution.py:21
  53.0 0.0 all-reduce.2.cloned.1.call-update
  53.0 0.0 reduce-scatter.6.cloned.1.call-start
  53.1 90.5 %all-reduce.2.cloned.1.call-done = bf16[512,1280]{1,0:T(8,128)(2,1)} async-done(((bf16[512,1280]{1,0:T(8,128)(2,1)}), bf16[512,1280]{1,0:T(8,128)(2,1)}) %all-reduce.2.cloned.1.call-update) | async-done | bytes 1310736 | tf_op jit(solution)/shard_map/psum | solution.py:22
  143.6 0.0 copy-done
  143.6 0.0 copy-done.3
  143.6 0.0 copy-done.2
  143.6 9.8 %convert_multiply_fusion = (f32[1728,1280]{1,0:T(8,128)}, f32[1728,1280]{1,0:T(8,128)}) fusion(bf16[1,1728,1280]{2,1,0:T(8,128)(2,1)} %param.5, bf16[512,1280]{1,0:T(8,128)(2,1)} %all-reduce.2.cloned.1.call-done, bf16[1,128,1280]{2,1,0:T(8,128)(2,1)S(1)} %copy-done, s32[512]{0:T(512)S(1)} %bitcast.33, bf16[1,512,1728]{1,2,0:T(8,128)(2,1)S(1)} %copy-done.2), kind=kOutput, calls=%fused_computation | convolution fusion | flops 2442461184 | bytes 25528320 | tf_op jit(solution)/shard_map/dot_general | solution.py:27
  153.4 0.0 reduce-scatter.6.cloned.1.call-update
  153.4 0.0 reduce-scatter.8.cloned.1.call-start
  153.4 0.5 reduce-scatter.8.cloned.1.call-update
  154.0 0.0 reduce-scatter.10.cloned.1.call-start
  154.0 96.8 %reduce-scatter.6.cloned.1.call-done = f32[216,1280]{1,0:T(8,128)} async-done(((f32[1728,1280]{1,0:T(8,128)}), f32[216,1280]{1,0:T(8,128)}) %reduce-scatter.6.cloned.1.call-update) | async-done | bytes 1105936 | tf_op jit(solution)/shard_map/reduce_scatter | solution.py:30
  250.8 104.8 %reduce-scatter.8.cloned.1.call-done = f32[216,1280]{1,0:T(8,128)} async-done(((f32[1728,1280]{1,0:T(8,128)}), f32[216,1280]{1,0:T(8,128)}) %reduce-scatter.8.cloned.1.call-update) | async-done | bytes 1105936 | tf_op jit(solution)/shard_map/reduce_scatter | solution.py:31
  355.7 1.7 divide_convert_fusion
  357.4 0.3 stack.2
  357.7 106.7 %all_to_all.5 = bf16[8,216,1280]{2,1,0:T(8,128)(2,1)S(1)} all-to-all(bf16[8,216,1280]{2,1,0:T(8,128)(2,1)S(1)} %stack.2), channel_id=1, replica_groups=mesh['task'=8,'row'=8,'col'=4] {'task'}, dimensions={0} | all-to-all | bytes 8847360 | tf_op jit(solution)/shard_map/all_to_all | solution.py:35
  464.4 0.0 copy-start.1
  464.4 2.0 copy-done.1
  466.4 2.6 fusion.7
  469.0 1.4 copy.8
  470.4 0.0 reduce-scatter.10.cloned.1.call-update
  470.5 41.1 %reduce-scatter.10.cloned.1.call-done = bf16[64,1280]{1,0:T(8,128)(2,1)} async-done(((bf16[512,1280]{1,0:T(8,128)(2,1)}), bf16[64,1280]{1,0:T(8,128)(2,1)}) %reduce-scatter.10.cloned.1.call-update) | async-done | bytes 163856
  511.6 1.1 copy.9
  512.7 0.8 copy.7
  513.5 4.6 copy.12
Async XLA Ops:
  7.2 136.4 %copy-start = (bf16[1,128,1280]{2,1,0:T(8,128)(2,1)S(1)}, bf16[1,128,1280]{2,1,0:T(8,128)(2,1)}, u32[]{:S(2)}) copy-start(bf16[1,128,1280]{2,1,0:T(8,128)(2,1)} %param.7) | copy-start | bytes 983044
  7.2 39.2 %all-gather.3.cloned.1.call-start = ((), (), s32[]{:S(2)}) async-start(), calls=%async_computation.7 | async-start | bytes 2211840 | tf_op jit(solution)/shard_map/all_gather | solution.py:20
  7.9 135.7 %copy-start.3 = (s32[1,512]{1,0:T(1,128)S(1)}, s32[1,512]{1,0:T(1,128)}, u32[]{:S(2)}) copy-start(s32[1,512]{1,0:T(1,128)} %param.6) | copy-start | bytes 6148
  7.9 135.7 %all-reduce.2.cloned.1.call-start = ((), (), s32[]{:S(2)}) async-start(), calls=%async_computation.4 | async-start | bytes 2621440 | tf_op jit(solution)/shard_map/psum | solution.py:22
  46.4 97.2 %copy-start.2 = (bf16[1,512,1728]{1,2,0:T(8,128)(2,1)S(1)}, bf16[1,512,1728]{1,2,0:T(8,128)(2,1)}, u32[]{:S(2)}) copy-start(bf16[1,512,1728]{1,2,0:T(8,128)(2,1)} %all-gather.3.cloned.1.call-done) | copy-start | bytes 5308420
  53.0 197.8 %reduce-scatter.6.cloned.1.call-start = ((), (), s32[]{:S(2)}) async-start(), calls=%async_computation.5 | async-start | bytes 9953280 | tf_op jit(solution)/shard_map/reduce_scatter | solution.py:30
  153.4 202.3 %reduce-scatter.8.cloned.1.call-start = ((), (), s32[]{:S(2)}) async-start(), calls=%async_computation.6 | async-start | bytes 9953280 | tf_op jit(solution)/shard_map/reduce_scatter | solution.py:31
  154.0 357.6 %reduce-scatter.10.cloned.1.call-start = ((), (), s32[]{:S(2)}) async-start(), calls=%async_computation.8 | async-start | bytes 1474560
  464.4 2.0 copy-start.1
Sparse Core Ops, SparseCore 0:
  9.8 36.5 all-gather.2
  53.1 90.4 all-reduce.1
  153.5 97.2 reduce-scatter.5
  253.5 102.1 reduce-scatter.7
  470.6 40.9 reduce-scatter.9
